TPU v7x, 32 devices: a whole 2x2x4 slice. The times are simulated.
32 devices in a mesh: dp: 8 (over z, y), tensor: 4 (over x, core).
Axes of the slice: x: 2, y: 2, z: 4, core: 2. Of those that a mesh axis runs over, the one named last changes fastest.
Arguments:
- inputs: bfloat16 [8192, 1536], P('dp', 'tensor'), may hold values from -6 to 6
- segment_ids: int32 [8192], P('dp'), may hold values from 0 to 26, never falling along the last dimension, each value on 1 to 1000 neighbouring positions
- cotangent: bfloat16 [8192, 1536], P('dp', 'tensor'), may hold values from -6 to 6
- first_gain: bfloat16 [1536], replicated, may hold values from 0.5 to 1.5
- gate_weight: bfloat16 [1536, 2048], P(None, 'tensor'), may hold values from -0.15625 to 0.15625
- gate_bias: bfloat16 [2048], P('tensor'), may hold values from -3 to 3
- branch_weight: bfloat16 [1536, 2048], P(None, 'tensor'), may hold values from -0.15625 to 0.15625
- branch_bias: bfloat16 [2048], P('tensor'), may hold values from -3 to 3
- conv_weight: bfloat16 [4, 2048], P(None, 'tensor'), may hold values from -3 to 3
- conv_bias: bfloat16 [2048], P('tensor'), may hold values from -3 to 3
- rate_weight: bfloat16 [16, 128, 128], P('tensor'), may hold values from -0.5 to 0.5
- rate_bias: bfloat16 [2048], P('tensor'), may hold values from -3 to 3
- input_weight: bfloat16 [16, 128, 128], P('tensor'), may hold values from -0.5 to 0.5
- input_bias: bfloat16 [2048], P('tensor'), may hold values from -3 to 3
- decay_param: float32 [2048], P('tensor'), may hold values from 3 to 7
- out_weight: bfloat16 [2048, 1536], P('tensor'), may hold values from -0.25 to 0.25
- second_gain: bfloat16 [1536], replicated, may hold values from 0.5 to 1.5
- ffn_gate: bfloat16 [1536, 4608], P(None, 'tensor'), may hold values from -0.15625 to 0.15625
- ffn_up: bfloat16 [1536, 4608], P(None, 'tensor'), may hold values from -0.15625 to 0.15625
- ffn_down: bfloat16 [4608, 1536], P('tensor'), may hold values from -0.1875 to 0.1875
Outputs:
- output: bfloat16 [8192, 1536], P('dp', 'tensor')
- input_grad: float32 [8192, 1536], P('dp', 'tensor')
- first_gain_grad: float32 [1536], replicated
- gate_weight_grad: float32 [1536, 2048], P(None, 'tensor')
- gate_bias_grad: float32 [2048], P('tensor')
- branch_weight_grad: float32 [1536, 2048], P(None, 'tensor')
- branch_bias_grad: float32 [2048], P('tensor')
- conv_weight_grad: float32 [4, 2048], P(None, 'tensor')
- conv_bias_grad: float32 [2048], P('tensor')
- rate_weight_grad: float32 [16, 128, 128], P('tensor')
- rate_bias_grad: float32 [2048], P('tensor')
- input_weight_grad: float32 [16, 128, 128], P('tensor')
- input_bias_grad: float32 [2048], P('tensor')
- decay_grad: float32 [2048], P('tensor')
- out_weight_grad: float32 [2048, 1536], P('tensor')
- second_gain_grad: float32 [1536], replicated
- ffn_gate_grad: float32 [1536, 4608], P(None, 'tensor')
- ffn_up_grad: float32 [1536, 4608], P(None, 'tensor')
- ffn_down_grad: float32 [4608, 1536], P('tensor')
Inputs may be any that keep to these rules, and one draw needn't show every extreme that they name: `segment_ids`: segment numbers never fall along the tokens; each document has 1 to 1000 consecutive tokens, one exactly 1000.
All inputs are finite; a program needn't handle non-finite values.
Results may differ from a plain program's by a relative error of at most 0.013.
Values may be sent and summed in bfloat16 or wider, within the bound.
A program may use at most 256 MiB of HBM per device.

v0:
```python
import jax
import jax.numpy as jnp
from jax import lax
from jax.sharding import PartitionSpec as P

SEQ = 1024
EPSILON = 1e-06
FLOOR = 0.05


def rms_scale(values, gain):
    return values * lax.rsqrt(jnp.mean(values * values, axis=-1, keepdims=True) + EPSILON) * gain


def seq_masks(segments, length):
    count = segments.shape[0]
    place = jnp.arange(count, dtype=jnp.int32) % length
    previous = jnp.concatenate([segments[:1], segments[:-1]])
    reset = (place == 0) | (segments != previous)
    return (place, reset)


def conv_apply(values, weights, shift_bias, segments, place):
    total = shift_bias + weights[0] * values
    for offset in range(1, weights.shape[0]):
        moved = jnp.concatenate(
            [jnp.zeros((offset, values.shape[1]), values.dtype), values[:-offset]]
        )
        earlier = jnp.concatenate([jnp.full((offset,), -1, jnp.int32), segments[:-offset]])
        usable = ((place >= offset) & (segments == earlier)).astype(values.dtype)
        total = total + weights[offset] * moved * usable[:, None]
    return total


def gates_to_step(rate_pre, input_pre, conv_out, decay, reset):
    rate = jax.nn.sigmoid(rate_pre)
    opened = jax.nn.sigmoid(input_pre)
    decayed = jnp.exp(-8.0 * rate * jax.nn.softplus(-decay))
    keep = jnp.where(reset[:, None], jnp.zeros_like(decayed), decayed)
    scale = jnp.where(
        reset[:, None],
        jnp.ones_like(decayed),
        jnp.sqrt(jnp.maximum(1.0 - decayed * decayed, FLOOR)),
    )
    return (keep, scale * opened * conv_out)


def combine(earlier, later):
    return (earlier[0] * later[0], later[0] * earlier[1] + later[1])


def block_mix(values, weight):
    rows = values.shape[0]
    split = values.reshape(rows, weight.shape[0], -1)
    return jnp.einsum("thi,hij->thj", split, weight, preferred_element_type=jnp.float32).reshape(
        rows, -1
    )


def block_back(grads, weight):
    rows = grads.shape[0]
    split = grads.reshape(rows, weight.shape[0], -1)
    return jnp.einsum("thj,hij->thi", split, weight, preferred_element_type=jnp.float32).reshape(
        rows, -1
    )


def block_grad(values, grads, heads):
    rows = values.shape[0]
    left = values.reshape(rows, heads, -1)
    right = grads.reshape(rows, heads, -1)
    return jnp.einsum("thi,thj->hij", left, right, preferred_element_type=jnp.float32)


def column_sum(values):
    return jnp.sum(values.astype(jnp.float32), axis=0)


def body(
    inputs,
    segment_ids,
    cotangent,
    first_gain,
    gate_weight,
    gate_bias,
    branch_weight,
    branch_bias,
    conv_weight,
    conv_bias,
    rate_weight,
    rate_bias,
    input_weight,
    input_bias,
    decay_param,
    out_weight,
    second_gain,
    ffn_gate,
    ffn_up,
    ffn_down,
):
    share = inputs.shape[1]
    heads = rate_weight.shape[0]
    offset = lax.axis_index("tensor") * share
    place, reset = seq_masks(segment_ids, SEQ)
    whole_in = lax.all_gather(inputs, "tensor", axis=1, tiled=True).astype(jnp.float32)
    normed_one, first_pull = jax.vjp(rms_scale, whole_in, first_gain.astype(jnp.float32))
    normed_low = normed_one.astype(jnp.bfloat16)
    gate_pre = jnp.dot(
        normed_low, gate_weight, preferred_element_type=jnp.float32
    ) + gate_bias.astype(jnp.float32)
    branch_pre = jnp.dot(
        normed_low, branch_weight, preferred_element_type=jnp.float32
    ) + branch_bias.astype(jnp.float32)

    def conv_local(values, weights, shift_bias):
        return conv_apply(values, weights, shift_bias, segment_ids, place)

    conv_out, conv_pull = jax.vjp(
        conv_local, branch_pre, conv_weight.astype(jnp.float32), conv_bias.astype(jnp.float32)
    )
    conv_low = conv_out.astype(jnp.bfloat16)
    rate_pre = block_mix(conv_low, rate_weight) + rate_bias.astype(jnp.float32)
    input_pre = block_mix(conv_low, input_weight) + input_bias.astype(jnp.float32)

    def step_local(rate_in, input_in, driven, decay):
        return gates_to_step(rate_in, input_in, driven, decay, reset)

    (keep, drive), step_pull = jax.vjp(step_local, rate_pre, input_pre, conv_out, decay_param)
    state = lax.associative_scan(combine, (keep, drive))[1]
    gate_act, gelu_pull = jax.vjp(jax.nn.gelu, gate_pre)
    mixed_low = (gate_act * state).astype(jnp.bfloat16)
    partial_value = jnp.dot(mixed_low, out_weight, preferred_element_type=jnp.float32)
    resid = whole_in + lax.psum(partial_value, "tensor")
    resid_mine = lax.dynamic_slice_in_dim(resid, offset, share, 1)
    normed_two, second_pull = jax.vjp(rms_scale, resid, second_gain.astype(jnp.float32))
    two_low = normed_two.astype(jnp.bfloat16)
    hidden_gate = jnp.dot(two_low, ffn_gate, preferred_element_type=jnp.float32)
    hidden_up = jnp.dot(two_low, ffn_up, preferred_element_type=jnp.float32)
    hidden_act, hidden_pull = jax.vjp(jax.nn.gelu, hidden_gate)
    hidden_low = (hidden_act * hidden_up).astype(jnp.bfloat16)
    ffn_part = jnp.dot(hidden_low, ffn_down, preferred_element_type=jnp.float32)
    output = (
        resid_mine
        + lax.psum_scatter(
            ffn_part.astype(jnp.bfloat16), "tensor", scatter_dimension=1, tiled=True
        ).astype(jnp.float32)
    ).astype(jnp.bfloat16)
    whole_cot = lax.all_gather(cotangent, "tensor", axis=1, tiled=True)
    d_hidden = jnp.einsum("td,fd->tf", whole_cot, ffn_down, preferred_element_type=jnp.float32)
    ffn_down_grad = jnp.einsum(
        "tf,td->fd", hidden_low, whole_cot, preferred_element_type=jnp.float32
    )
    d_hgate = hidden_pull(d_hidden * hidden_up)[0].astype(jnp.bfloat16)
    d_hup = (d_hidden * hidden_act).astype(jnp.bfloat16)
    ffn_gate_grad = jnp.einsum("td,tf->df", two_low, d_hgate, preferred_element_type=jnp.float32)
    ffn_up_grad = jnp.einsum("td,tf->df", two_low, d_hup, preferred_element_type=jnp.float32)
    d_two_part = jnp.einsum(
        "tf,df->td", d_hgate, ffn_gate, preferred_element_type=jnp.float32
    ) + jnp.einsum("tf,df->td", d_hup, ffn_up, preferred_element_type=jnp.float32)
    d_two = lax.psum(d_two_part, "tensor")
    d_resid_norm, second_gain_grad = second_pull(d_two)
    d_resid = whole_cot.astype(jnp.float32) + d_resid_norm
    d_resid_low = d_resid.astype(jnp.bfloat16)
    out_weight_grad = jnp.einsum(
        "tr,td->rd", mixed_low, d_resid_low, preferred_element_type=jnp.float32
    )
    d_mixed = jnp.einsum("td,rd->tr", d_resid_low, out_weight, preferred_element_type=jnp.float32)
    d_gate_low = gelu_pull(d_mixed * state)[0].astype(jnp.bfloat16)
    d_state = d_mixed * gate_act
    channels = keep.shape[1]
    keep_next = jnp.concatenate([keep[1:], jnp.zeros((1, channels), jnp.float32)])
    adjoint = lax.associative_scan(combine, (keep_next, d_state), reverse=True)[1]
    state_prev = jnp.concatenate([jnp.zeros((1, channels), jnp.float32), state[:-1]])
    d_rate, d_input, d_conv_direct, decay_grad = step_pull((adjoint * state_prev, adjoint))
    d_rate_low = d_rate.astype(jnp.bfloat16)
    d_input_low = d_input.astype(jnp.bfloat16)
    rate_weight_grad = block_grad(conv_low, d_rate_low, heads)
    input_weight_grad = block_grad(conv_low, d_input_low, heads)
    rate_bias_grad = column_sum(d_rate_low)
    input_bias_grad = column_sum(d_input_low)
    d_conv = (
        d_conv_direct + block_back(d_rate_low, rate_weight) + block_back(d_input_low, input_weight)
    )
    d_branch, conv_weight_grad, conv_bias_grad = conv_pull(d_conv)
    d_branch_low = d_branch.astype(jnp.bfloat16)
    gate_weight_grad = jnp.einsum(
        "td,tr->dr", normed_low, d_gate_low, preferred_element_type=jnp.float32
    )
    branch_weight_grad = jnp.einsum(
        "td,tr->dr", normed_low, d_branch_low, preferred_element_type=jnp.float32
    )
    gate_bias_grad = column_sum(d_gate_low)
    branch_bias_grad = column_sum(d_branch_low)
    d_first_part = jnp.einsum(
        "tr,dr->td", d_gate_low, gate_weight, preferred_element_type=jnp.float32
    ) + jnp.einsum("tr,dr->td", d_branch_low, branch_weight, preferred_element_type=jnp.float32)
    d_first = lax.psum(d_first_part.astype(jnp.bfloat16), "tensor").astype(jnp.float32)
    d_in_norm, first_gain_grad = first_pull(d_first)
    input_grad = lax.dynamic_slice_in_dim(d_resid + d_in_norm, offset, share, 1)
    pieces = (
        lax.psum_scatter(first_gain_grad, "dp", scatter_dimension=0, tiled=True),
        lax.psum_scatter(gate_weight_grad, "dp", scatter_dimension=0, tiled=True),
        lax.psum_scatter(gate_bias_grad, "dp", scatter_dimension=0, tiled=True),
        lax.psum_scatter(branch_weight_grad, "dp", scatter_dimension=0, tiled=True),
        lax.psum_scatter(branch_bias_grad, "dp", scatter_dimension=0, tiled=True),
        lax.psum_scatter(conv_weight_grad, "dp", scatter_dimension=1, tiled=True),
        lax.psum_scatter(conv_bias_grad, "dp", scatter_dimension=0, tiled=True),
        lax.psum_scatter(rate_weight_grad, "dp", scatter_dimension=1, tiled=True),
        lax.psum_scatter(rate_bias_grad, "dp", scatter_dimension=0, tiled=True),
        lax.psum_scatter(input_weight_grad, "dp", scatter_dimension=1, tiled=True),
        lax.psum_scatter(input_bias_grad, "dp", scatter_dimension=0, tiled=True),
        lax.psum_scatter(decay_grad, "dp", scatter_dimension=0, tiled=True),
        lax.psum_scatter(out_weight_grad, "dp", scatter_dimension=0, tiled=True),
        lax.psum_scatter(second_gain_grad, "dp", scatter_dimension=0, tiled=True),
        lax.psum_scatter(ffn_gate_grad, "dp", scatter_dimension=0, tiled=True),
        lax.psum_scatter(ffn_up_grad, "dp", scatter_dimension=0, tiled=True),
        lax.psum_scatter(ffn_down_grad, "dp", scatter_dimension=1, tiled=True),
    )
    done = (
        lax.all_gather(pieces[0].astype(jnp.bfloat16), "dp", axis=0, tiled=True).astype(
            jnp.float32
        ),
        lax.all_gather(pieces[1].astype(jnp.bfloat16), "dp", axis=0, tiled=True).astype(
            jnp.float32
        ),
        lax.all_gather(pieces[2].astype(jnp.bfloat16), "dp", axis=0, tiled=True).astype(
            jnp.float32
        ),
        lax.all_gather(pieces[3].astype(jnp.bfloat16), "dp", axis=0, tiled=True).astype(
            jnp.float32
        ),
        lax.all_gather(pieces[4].astype(jnp.bfloat16), "dp", axis=0, tiled=True).astype(
            jnp.float32
        ),
        lax.all_gather(pieces[5].astype(jnp.bfloat16), "dp", axis=1, tiled=True).astype(
            jnp.float32
        ),
        lax.all_gather(pieces[6].astype(jnp.bfloat16), "dp", axis=0, tiled=True).astype(
            jnp.float32
        ),
        lax.all_gather(pieces[7].astype(jnp.bfloat16), "dp", axis=1, tiled=True).astype(
            jnp.float32
        ),
        lax.all_gather(pieces[8].astype(jnp.bfloat16), "dp", axis=0, tiled=True).astype(
            jnp.float32
        ),
        lax.all_gather(pieces[9].astype(jnp.bfloat16), "dp", axis=1, tiled=True).astype(
            jnp.float32
        ),
        lax.all_gather(pieces[10].astype(jnp.bfloat16), "dp", axis=0, tiled=True).astype(
            jnp.float32
        ),
        lax.all_gather(pieces[11].astype(jnp.bfloat16), "dp", axis=0, tiled=True).astype(
            jnp.float32
        ),
        lax.all_gather(pieces[12].astype(jnp.bfloat16), "dp", axis=0, tiled=True).astype(
            jnp.float32
        ),
        lax.all_gather(pieces[13].astype(jnp.bfloat16), "dp", axis=0, tiled=True).astype(
            jnp.float32
        ),
        lax.all_gather(pieces[14].astype(jnp.bfloat16), "dp", axis=0, tiled=True).astype(
            jnp.float32
        ),
        lax.all_gather(pieces[15].astype(jnp.bfloat16), "dp", axis=0, tiled=True).astype(
            jnp.float32
        ),
        lax.all_gather(pieces[16].astype(jnp.bfloat16), "dp", axis=1, tiled=True).astype(
            jnp.float32
        ),
    )
    return (
        output,
        input_grad,
        done[0],
        done[1],
        done[2],
        done[3],
        done[4],
        done[5],
        done[6],
        done[7],
        done[8],
        done[9],
        done[10],
        done[11],
        done[12],
        done[13],
        done[14],
        done[15],
        done[16],
    )


def solution(mesh):
    in_specs = (
        P("dp", "tensor"),
        P("dp"),
        P("dp", "tensor"),
        P(),
        P(None, "tensor"),
        P("tensor"),
        P(None, "tensor"),
        P("tensor"),
        P(None, "tensor"),
        P("tensor"),
        P("tensor", None, None),
        P("tensor"),
        P("tensor", None, None),
        P("tensor"),
        P("tensor"),
        P("tensor", None),
        P(),
        P(None, "tensor"),
        P(None, "tensor"),
        P("tensor", None),
    )
    out_specs = (
        P("dp", "tensor"),
        P("dp", "tensor"),
        P(),
        P(None, "tensor"),
        P("tensor"),
        P(None, "tensor"),
        P("tensor"),
        P(None, "tensor"),
        P("tensor"),
        P("tensor", None, None),
        P("tensor"),
        P("tensor", None, None),
        P("tensor"),
        P("tensor"),
        P("tensor", None),
        P(),
        P(None, "tensor"),
        P(None, "tensor"),
        P("tensor", None),
    )
    return jax.shard_map(body, mesh=mesh, in_specs=in_specs, out_specs=out_specs, check_vma=False)
```

profile of v0, /device:TPU:0, one launch (start us, length us, event | category | flops | bytes accessed | tf_op | source)
XLA Modules:
  0.0 2209.8 jit_solution(8797544625298831027)
XLA Ops:
  21.3 19.5 all-gather.10.cloned.1.call-done
  70.8 6.3 slice.535
  77.0 6.3 slice.536
  83.3 6.3 slice.534
  89.5 6.3 slice.538
  207.6 6.3 slice.533
  214.0 6.3 slice.606
  284.1 8.6 pad.169
  296.5 8.6 pad.168
  305.1 8.0 multiply_convert_fusion.4
  319.4 118.9 %all-reduce.76.cloned.1.call-done = f32[1024,1536]{1,0:T(8,128)} async-done(((f32[1024,1536]{1,0:T(8,128)}), f32[1024,1536]{1,0:T(8,128)}) %all-reduce.76.cloned.1.call-update) | async-done | bytes 6291472 | tf_op jit(solution)/shard_map/psum | solution.py:133
  447.3 5.8 fusion.119
  453.1 5.8 fusion.120
  458.9 9.7 all-gather.12.cloned.1.call-done
  468.6 12.3 multiply_convert_fusion.2
  485.2 6.2 convolution_add_fusion
  494.9 6.7 slice.611
  501.6 6.2 slice.618
  507.8 6.3 slice.609
  514.1 8.9 slice.612
  523.0 8.9 slice.619
  531.8 9.1 slice.610
  545.0 66.2 %all-reduce.78.cloned.1.call-done = f32[1024,1536]{1,0:T(8,128)} async-done(((f32[1024,1536]{1,0:T(8,128)}), f32[1024,1536]{1,0:T(8,128)}) %all-reduce.78.cloned.1.call-update) | async-done | bytes 6291472 | tf_op jit(solution)/shard_map/psum | solution.py:160
  611.2 6.3 multiply_reduce_fusion
  628.3 6.3 slice.613
  634.5 6.2 slice.615
  640.8 8.9 slice.614
  649.7 8.9 slice.616
  770.3 6.2 slice.687
  840.5 8.5 pad.189
  849.0 9.1 slice.688
  861.9 8.5 pad.188
  874.5 16.6 rev.2
  891.1 8.4 multiply_reduce_fusion.5
  913.1 6.7 multiply_reduce_fusion.9
  930.1 6.6 fusion.24
  936.8 5.9 fusion.86
  942.8 9.9 fusion.123
  952.8 10.0 fusion.124
  963.2 9.9 fusion.125
  980.9 6.1 fusion.122
  987.1 7.3 add_convert_fusion
  994.5 7.3 convolution_convert_fusion
  1008.3 73.4 %reduce-scatter.23.cloned.1.call-done = f32[64,1536]{1,0:T(8,128)} async-done(((f32[512,1536]{1,0:T(8,128)}), f32[64,1536]{1,0:T(8,128)}) %reduce-scatter.23.cloned.1.call-update) | async-done | bytes 393232 | tf_op jit(solution)/shard_map/reduce_scatter | solution.py:213
  1083.5 75.9 %reduce-scatter.15.cloned.1.call-done = f32[192,512]{1,0:T(8,128)} async-done(((f32[1536,512]{1,0:T(8,128)}), f32[192,512]{1,0:T(8,128)}) %reduce-scatter.15.cloned.1.call-update) | async-done | bytes 393232 | tf_op jit(solution)/shard_map/reduce_scatter | solution.py:202
  1161.3 130.8 %reduce-scatter.25.cloned.1.call-done = f32[192,1152]{1,0:T(8,128)} async-done(((f32[1536,1152]{1,0:T(8,128)}), f32[192,1152]{1,0:T(8,128)}) %reduce-scatter.25.cloned.1.call-update) | async-done | bytes 884752 | tf_op jit(solution)/shard_map/reduce_scatter | solution.py:215
  1294.1 130.5 %reduce-scatter.27.cloned.1.call-done = f32[192,1152]{1,0:T(8,128)} async-done(((f32[1536,1152]{1,0:T(8,128)}), f32[192,1152]{1,0:T(8,128)}) %reduce-scatter.27.cloned.1.call-update) | async-done | bytes 884752 | tf_op jit(solution)/shard_map/reduce_scatter | solution.py:216
  1426.7 130.4 %reduce-scatter.29.cloned.1.call-done = f32[1152,192]{0,1:T(8,128)} async-done(((f32[1152,1536]{0,1:T(8,128)}), f32[1152,192]{0,1:T(8,128)}) %reduce-scatter.29.cloned.1.call-update) | async-done | bytes 884752 | tf_op jit(solution)/shard_map/reduce_scatter | solution.py:217
  1567.7 54.5 %reduce-scatter.33.cloned.1.call-done = f32[64,4]{1,0:T(8,128)} async-done(((f32[512,4]{1,0:T(8,128)}), f32[64,4]{1,0:T(8,128)}) %reduce-scatter.33.cloned.1.call-update) | async-done | bytes 1040
  1623.0 18.6 all-gather
  1642.3 45.2 %reduce-scatter.19.cloned.1.call-done = f32[4,16,128]{2,1,0:T(8,128)} async-done(((f32[4,128,128]{2,1,0:T(8,128)}), f32[4,16,128]{2,1,0:T(8,128)}) %reduce-scatter.19.cloned.1.call-update) | async-done | bytes 32784 | tf_op jit(solution)/shard_map/reduce_scatter | solution.py:208
  1688.3 30.6 %all_gather.66 = bf16[4,128,128]{2,1,0:T(8,128)(2,1)S(1)} all-gather(bf16[4,16,128]{2,1,0:T(8,128)(2,1)S(1)} %convert_element_type.250), channel_id=1, replica_groups=mesh['dp'=8,'tensor'=4] {'dp'}, dimensions={1}, use_global_device_ids=true | all-gather | bytes 147456 | tf_op jit(solution)/shard_map/all_gather | solution.py:241
  1719.6 33.4 %reduce-scatter.21.cloned.1.call-done = f32[4,16,128]{2,1,0:T(8,128)} async-done(((f32[4,128,128]{2,1,0:T(8,128)}), f32[4,16,128]{2,1,0:T(8,128)}) %reduce-scatter.21.cloned.1.call-update) | async-done | bytes 32784 | tf_op jit(solution)/shard_map/reduce_scatter | solution.py:210
  1753.7 30.8 %all_gather.68 = bf16[4,128,128]{2,1,0:T(8,128)(2,1)S(1)} all-gather(bf16[4,16,128]{2,1,0:T(8,128)(2,1)S(1)} %convert_element_type.255), channel_id=1, replica_groups=mesh['dp'=8,'tensor'=4] {'dp'}, dimensions={1}, use_global_device_ids=true | all-gather | bytes 147456 | tf_op jit(solution)/shard_map/all_gather | solution.py:247
  1785.2 38.1 %all-reduce.80.cloned.1.call-done = bf16[1024,1536]{1,0:T(8,128)(2,1)} async-done(((bf16[1024,1536]{1,0:T(8,128)(2,1)}), bf16[1024,1536]{1,0:T(8,128)(2,1)}) %all-reduce.80.cloned.1.call-update) | async-done | bytes 3145744 | tf_op jit(solution)/shard_map/psum | solution.py:197
  1823.3 6.8 fusion
  1830.2 38.4 %all-reduce.70 = (bf16[1536]{0:T(1024)(128)(2,1)}, bf16[512]{0:T(512)(128)(2,1)}, bf16[512]{0:T(512)(128)(2,1)}, bf16[512]{0:T(512)(128)(2,1)}, bf16[512]{0:T(51...) all-reduce(f32[1536]{0:T(1024)} %get-tuple-element.116, ...), channel_id=3, replica_groups=mesh['dp'=8,'tensor'=4] {'dp'}, use_global_device_ids=true, to_apply=%region_9.10.clone | all-reduce | flops 6144 | bytes 36864
  1887.8 34.5 %all-reduce.71 = (bf16[1536]{0:T(1024)(128)(2,1)}, bf16[512]{0:T(512)(128)(2,1)}, bf16[512]{0:T(512)(128)(2,1)}, bf16[512]{0:T(512)(128)(2,1)}, bf16[512]{0:T(51...) all-reduce(bf16[1536]{0:T(1024)(128)(2,1)S(1)} %dynamic-update-slic, ...), channel_id=1, replica_groups=mesh['dp'=8,'tensor'=4] {'dp'}, use_global_device_ids=true, to_apply=%add.54 | all-reduce | flops 6144 | bytes 24576
  1945.6 10.5 all-gather.18.cloned.1.call-done
  1959.6 41.1 %all-gather.14.cloned.1.call-done = bf16[1536,512]{1,0:T(8,128)(2,1)} async-done(((bf16[192,512]{1,0:T(8,128)(2,1)}), bf16[1536,512]{1,0:T(8,128)(2,1)}) %all-gather.14.cloned.1.call-update) | async-done | bytes 1572880 | tf_op jit(solution)/shard_map/all_gather | solution.py:223
  2004.2 61.7 %all-gather.20.cloned.1.call-done = bf16[1536,1152]{1,0:T(8,128)(2,1)} async-done(((bf16[192,1152]{1,0:T(8,128)(2,1)}), bf16[1536,1152]{1,0:T(8,128)(2,1)}) %all-gather.20.cloned.1.call-update) | async-done | bytes 3538960 | tf_op jit(solution)/shard_map/all_gather | solution.py:262
  2071.3 60.0 %all-gather.22.cloned.1.call-done = bf16[1536,1152]{1,0:T(8,128)(2,1)} async-done(((bf16[192,1152]{1,0:T(8,128)(2,1)}), bf16[1536,1152]{1,0:T(8,128)(2,1)}) %all-gather.22.cloned.1.call-update) | async-done | bytes 3538960 | tf_op jit(solution)/shard_map/all_gather | solution.py:265
  2136.7 60.1 %all-gather.24.cloned.1.call-done = bf16[1152,1536]{0,1:T(8,128)(2,1)} async-done(((bf16[1152,192]{0,1:T(8,128)(2,1)}), bf16[1152,1536]{0,1:T(8,128)(2,1)}) %all-gather.24.cloned.1.call-update) | async-done | bytes 3538960 | tf_op jit(solution)/shard_map/all_gather | solution.py:268
  2196.8 6.0 copy.116
  (525 shorter events, 563.4 us)
Async XLA Ops:
  7.2 461.4 %copy-start = (bf16[1152,1536]{1,0:T(8,128)(2,1)S(1)}, bf16[1152,1536]{1,0:T(8,128)(2,1)}, u32[]{:S(2)}) copy-start(bf16[1152,1536]{1,0:T(8,128)(2,1)} %param.39) | copy-start | bytes 10616836
  7.2 33.6 %all-gather.10.cloned.1.call-start = ((), (), s32[]{:S(2)}) async-start(), calls=%async_computation.10 | async-start | bytes 3932160 | tf_op jit(solution)/shard_map/all_gather | solution.py:105
  7.9 430.4 %all-reduce.76.cloned.1.call-start = ((), (), s32[]{:S(2)}) async-start(), calls=%async_computation.11 | async-start | bytes 12582912 | tf_op jit(solution)/shard_map/psum | solution.py:133
  13.9 51.3 %copy-start.15 = (f32[512]{0:T(512)}, f32[512]{0:T(512)S(1)}, u32[]{:S(2)}) copy-start(f32[512]{0:T(512)S(1)} %convert_element_type.215) | copy-start | bytes 6148
  21.3 26.2 %copy-start.17 = (f32[1024]{0:T(1024)}, f32[1024]{0:T(1024)S(1)}, u32[]{:S(2)}) copy-start(f32[1024]{0:T(1024)S(1)} %get-tuple-element.209) | copy-start | bytes 12292
  21.3 26.2 %copy-start.19 = (f32[1024]{0:T(1024)}, f32[1024]{0:T(1024)S(1)}, u32[]{:S(2)}) copy-start(f32[1024]{0:T(1024)S(1)} %get-tuple-element.214) | copy-start | bytes 12292
  21.3 26.2 %copy-start.21 = (f32[1024]{0:T(1024)}, f32[1024]{0:T(1024)S(1)}, u32[]{:S(2)}) copy-start(f32[1024]{0:T(1024)S(1)} %get-tuple-element.215) | copy-start | bytes 12292
  207.6 14.0 copy-start.45
  207.6 14.0 copy-start.59
  234.8 18.4 copy-start.55
  253.2 11.0 copy-start.53
  296.5 8.6 copy-start.24
  296.5 8.6 copy-start.31
  296.5 8.6 copy-start.64
  305.1 9.0 copy-start.74
  318.6 150.0 %all-gather.12.cloned.1.call-start = ((), (), s32[]{:S(2)}) async-start(), calls=%async_computation.12 | async-start | bytes 3932160 | tf_op jit(solution)/shard_map/all_gather | solution.py:148
  319.3 291.9 %all-reduce.78.cloned.1.call-start = ((), (), s32[]{:S(2)}) async-start(), calls=%async_computation.13 | async-start | bytes 12582912 | tf_op jit(solution)/shard_map/psum | solution.py:160
  442.9 4.4 copy-start.70
  447.3 5.8 copy-start.12
  447.3 5.8 copy-start.72
  468.6 12.3 copy-start.71
  480.9 4.3 copy-start.79
  480.9 4.3 copy-start.78
  480.9 4.3 copy-start.73
  491.5 515.1 %reduce-scatter.17.cloned.1.call-start = ((), (), s32[]{:S(2)}) async-start(), calls=%async_computation.17 | async-start | bytes 3538944 | tf_op jit(solution)/shard_map/reduce_scatter | solution.py:204
  611.2 6.4 copy-start.8
  611.2 7.4 copy-start.11
  618.6 4.6 copy-start.77
  622.5 5.8 copy-start.7
  761.6 16.2 copy-start.46
  761.6 16.3 copy-start.60
  791.0 18.4 copy-start.56
  809.5 11.0 copy-start.54
  874.5 16.6 copy-start.16
  874.5 16.6 copy-start.34
  874.5 16.6 copy-start.36
  874.5 16.6 copy-start.48
  891.1 8.4 copy-start.61
  891.1 9.0 copy-start.4
  913.1 6.8 copy-start.2
  913.1 6.8 copy-start.18
  913.1 6.7 copy-start.20
  929.9 151.9 %reduce-scatter.23.cloned.1.call-start = ((), (), s32[]{:S(2)}) async-start(), calls=%async_computation.21 | async-start | bytes 3538944 | tf_op jit(solution)/shard_map/reduce_scatter | solution.py:213
  936.7 222.8 %reduce-scatter.15.cloned.1.call-start = ((), (), s32[]{:S(2)}) async-start(), calls=%async_computation.15 | async-start | bytes 3538944 | tf_op jit(solution)/shard_map/reduce_scatter | solution.py:202
  942.7 349.3 %reduce-scatter.25.cloned.1.call-start = ((), (), s32[]{:S(2)}) async-start(), calls=%async_computation.23 | async-start | bytes 7962624 | tf_op jit(solution)/shard_map/reduce_scatter | solution.py:215
  952.7 471.9 %reduce-scatter.27.cloned.1.call-start = ((), (), s32[]{:S(2)}) async-start(), calls=%async_computation.25 | async-start | bytes 7962624 | tf_op jit(solution)/shard_map/reduce_scatter | solution.py:216
  962.8 594.3 %reduce-scatter.29.cloned.1.call-start = ((), (), s32[]{:S(2)}) async-start(), calls=%async_computation.27 | async-start | bytes 7962624 | tf_op jit(solution)/shard_map/reduce_scatter | solution.py:217
  973.2 649.0 %reduce-scatter.33.cloned.1.call-start = ((), (), s32[]{:S(2)}) async-start(), calls=%async_computation.30 | async-start | bytes 294912
  975.4 712.1 %reduce-scatter.19.cloned.1.call-start = ((), (), s32[]{:S(2)}) async-start(), calls=%async_computation.19 | async-start | bytes 294912 | tf_op jit(solution)/shard_map/reduce_scatter | solution.py:208
  978.2 774.8 %reduce-scatter.21.cloned.1.call-start = ((), (), s32[]{:S(2)}) async-start(), calls=%async_computation.20 | async-start | bytes 294912 | tf_op jit(solution)/shard_map/reduce_scatter | solution.py:210
  987.1 836.3 %all-reduce.80.cloned.1.call-start = ((), (), s32[]{:S(2)}) async-start(), calls=%async_computation.14 | async-start | bytes 6291456 | tf_op jit(solution)/shard_map/psum | solution.py:197
  994.5 942.5 %reduce-scatter.31.cloned.1.call-start = ((), (), s32[]{:S(2)}) async-start(), calls=%async_computation.29 | async-start | bytes 3932160
  1006.5 935.6 %all-gather.16.cloned.1.call-start = ((), (), s32[]{:S(2)}) async-start(), calls=%async_computation.18 | async-start | bytes 1769472 | tf_op jit(solution)/shard_map/all_gather | solution.py:229
  1008.3 947.8 %all-gather.18.cloned.1.call-start = ((), (), s32[]{:S(2)}) async-start(), calls=%async_computation.22 | async-start | bytes 1769472 | tf_op jit(solution)/shard_map/all_gather | solution.py:256
  1083.5 917.2 %all-gather.14.cloned.1.call-start = ((), (), s32[]{:S(2)}) async-start(), calls=%async_computation.16 | async-start | bytes 1769472 | tf_op jit(solution)/shard_map/all_gather | solution.py:223
  1161.2 904.7 %all-gather.20.cloned.1.call-start = ((), (), s32[]{:S(2)}) async-start(), calls=%async_computation.24 | async-start | bytes 3981312 | tf_op jit(solution)/shard_map/all_gather | solution.py:262
  1294.1 265.0 %copy-start.63 = (u32[32]{0:T(128)S(1)}, u32[32]{0:T(128)}, u32[]{:S(2)}) copy-start(u32[32]{0:T(128)} %constant.193) | copy-start | bytes 388
  1294.1 837.2 %all-gather.22.cloned.1.call-start = ((), (), s32[]{:S(2)}) async-start(), calls=%async_computation.26 | async-start | bytes 3981312 | tf_op jit(solution)/shard_map/all_gather | solution.py:265
  1426.6 770.2 %all-gather.24.cloned.1.call-start = ((), (), s32[]{:S(2)}) async-start(), calls=%async_computation.28 | async-start | bytes 3981312 | tf_op jit(solution)/shard_map/all_gather | solution.py:268
  1785.2 45.0 %copy-start.29 = (f32[1536]{0:T(1024)S(1)}, f32[1536]{0:T(1024)}, u32[]{:S(2)}) copy-start(f32[1536]{0:T(1024)} %get-tuple-element.114) | copy-start | bytes 18436
  1785.2 147.2 %copy-start.28 = (f32[1024]{0:T(1024)S(1)}, f32[1024]{0:T(1024)}, u32[]{:S(2)}) copy-start(f32[1024]{0:T(1024)} %copy-done.27) | copy-start | bytes 12292
  1785.2 147.9 %copy-start.26 = (f32[1024]{0:T(1024)S(1)}, f32[1024]{0:T(1024)}, u32[]{:S(2)}) copy-start(f32[1024]{0:T(1024)} %copy-done.23) | copy-start | bytes 12292
  1878.2 5.2 copy-start.68
  1879.0 6.6 copy-start.69
  (37 other events, 93.8 us)
Sparse Core Ops, SparseCore 0:
  9.6 31.1 all-gather.9
  318.7 119.5 all-reduce.75
  439.9 28.6 all-gather.11
  491.6 119.5 all-reduce.77
  930.0 74.7 reduce-scatter.16
  1008.2 73.4 reduce-scatter.22
  1085.3 74.0 reduce-scatter.14
  1163.7 128.2 reduce-scatter.24
  1296.3 128.2 reduce-scatter.26
  1428.7 128.2 reduce-scatter.28
  1560.9 61.1 reduce-scatter.32
  1625.9 61.5 reduce-scatter.18
  1691.4 61.5 reduce-scatter.20
  1755.8 67.5 all-reduce.79
  1826.3 37.9 reduce-scatter.30
  1866.9 44.3 all-gather.15
  1913.4 42.6 all-gather.17
  1958.1 42.5 all-gather.13
  2002.9 62.9 all-gather.19
  2067.9 63.3 all-gather.21
  2133.5 63.3 all-gather.23
where the time goes:
time: 2230 us; the launch traced here: 2210 us
  waiting for transfers between devices  1160 us (52%)
  local copies, waits for them, and re-layouts  501 us (22%)
  other arithmetic  237 us (11%)
  blocking collectives  153 us (7%)
  matrix products  138 us (6%)
    slice x66, local copies, waits for them, and re-layouts, body(): lax.associative_scan(combine, (keep_next, d_state), reverse=True)[1]  185 us
    slice x60, local copies, waits for them, and re-layouts, body(): state = lax.associative_scan(combine, (keep, drive))[1]  131 us
    reduce_scatter x1, waiting for transfers between devices, body(): lax.psum_scatter(ffn_gate_grad, 'dp', scatter_dimension=0, tiled=True)  131 us
    reduce_scatter x1, waiting for transfers between devices, body(): lax.psum_scatter(ffn_up_grad, 'dp', scatter_dimension=0, tiled=True)  130 us
    reduce_scatter x1, waiting for transfers between devices, body(): lax.psum_scatter(ffn_down_grad, 'dp', scatter_dimension=1, tiled=True)  130 us
    psum x1, waiting for transfers between devices, body(): resid = whole_in + lax.psum(partial_value, 'tensor')  119 us
    reduce_scatter x1, waiting for transfers between devices, body(): lax.psum_scatter(gate_weight_grad, 'dp', scatter_dimension=0, tiled=True)  75.9 us
    reduce_scatter x1, waiting for transfers between devices, body(): lax.psum_scatter(out_weight_grad, 'dp', scatter_dimension=0, tiled=True)  73.4 us
  transfers between devices with their start and end apart: 21, of which 18 were waited for; matrix products, arithmetic and copies ran while one was open for 11% of the time, Pallas kernels for 0%

commit v1 on v0

--- a/solution.py
+++ b/solution.py
@@ -1,3 +1,4 @@
+import functools
 import jax
 import jax.numpy as jnp
 from jax import lax
@@ -6,6 +7,14 @@
 SEQ = 1024
 EPSILON = 1e-06
 FLOOR = 0.05
+
+
+def shape_vector_over_axis(inp, axis_key):
+    extra = lax.all_gather(inp, axis_name=axis_key).sum(axis=0)
+    return extra
+
+
+handle_sections_over_axis = functools.partial(shape_vector_over_axis, axis_key="tensor")
 
 
 def rms_scale(values, gain):
@@ -130,7 +139,7 @@
     gate_act, gelu_pull = jax.vjp(jax.nn.gelu, gate_pre)
     mixed_low = (gate_act * state).astype(jnp.bfloat16)
     partial_value = jnp.dot(mixed_low, out_weight, preferred_element_type=jnp.float32)
-    resid = whole_in + lax.psum(partial_value, "tensor")
+    resid = whole_in + handle_sections_over_axis(partial_value)
     resid_mine = lax.dynamic_slice_in_dim(resid, offset, share, 1)
     normed_two, second_pull = jax.vjp(rms_scale, resid, second_gain.astype(jnp.float32))
     two_low = normed_two.astype(jnp.bfloat16)

time: 2230 us -> 2270 us (1.018)
  waiting for transfers between devices: 1160 us -> 1190 us
    all_gather x0 -> x1, waiting for transfers between devices: none -> 154 us  [shape_vector_over_axis(): extra = lax.all_gather(inp, axis_name=axis_key).sum(axis=0)]
    psum x1 -> x0, waiting for transfers between devices: 119 us -> none  [body(): resid = whole_in + lax.psum(partial_value, 'tensor')]
  transfers between devices with their start and end apart: 21 -> 21, of which waited for: 18 -> 17; matrix products, arithmetic and copies ran while one was open for 11% -> 12% of each run, Pallas kernels for 0% -> 0%
where the time goes in v1:
time: 2270 us; the launch traced here: 2250 us
  waiting for transfers between devices  1190 us (52%)
  local copies, waits for them, and re-layouts  501 us (22%)
  other arithmetic  250 us (11%)
  blocking collectives  153 us (7%)
  matrix products  138 us (6%)
    slice x66, local copies, waits for them, and re-layouts, body(): lax.associative_scan(combine, (keep_next, d_state), reverse=True)[1]  185 us
    all_gather x1, waiting for transfers between devices, shape_vector_over_axis(): extra = lax.all_gather(inp, axis_name=axis_key).sum(axis=0)  154 us
    slice x60, local copies, waits for them, and re-layouts, body(): state = lax.associative_scan(combine, (keep, drive))[1]  131 us
    reduce_scatter x1, waiting for transfers between devices, body(): lax.psum_scatter(ffn_gate_grad, 'dp', scatter_dimension=0, tiled=True)  131 us
    reduce_scatter x1, waiting for transfers between devices, body(): lax.psum_scatter(ffn_up_grad, 'dp', scatter_dimension=0, tiled=True)  130 us
    reduce_scatter x1, waiting for transfers between devices, body(): lax.psum_scatter(ffn_down_grad, 'dp', scatter_dimension=1, tiled=True)  130 us
    reduce_scatter x1, waiting for transfers between devices, body(): lax.psum_scatter(gate_weight_grad, 'dp', scatter_dimension=0, tiled=True)  75.4 us
    reduce_scatter x1, waiting for transfers between devices, body(): lax.psum_scatter(out_weight_grad, 'dp', scatter_dimension=0, tiled=True)  73.4 us
  transfers between devices with their start and end apart: 21, of which 17 were waited for; matrix products, arithmetic and copies ran while one was open for 12% of the time, Pallas kernels for 0%

profile of v1, /device:TPU:0, one launch (start us, length us, event | category | flops | bytes accessed | tf_op | source)
XLA Modules:
  0.0 2248.2 jit_solution(16707874555614285354)
XLA Ops:
  21.2 19.6 all-gather.12.cloned.1.call-done
  70.8 6.3 slice.535
  77.0 6.3 slice.536
  83.3 6.3 slice.534
  89.6 6.3 slice.538
  207.7 6.3 slice.533
  214.0 6.3 slice.606
  284.1 8.6 pad.169
  296.5 8.6 pad.168
  305.1 8.1 multiply_convert_fusion.4
  319.4 154.1 %all-gather.28.cloned.1.call-done = f32[4096,1536]{1,0:T(8,128)} async-done(((f32[1024,1536]{1,0:T(8,128)}), f32[4096,1536]{1,0:T(8,128)}) %all-gather.28.cloned.1.call-update) | async-done | bytes 25165840 | tf_op jit(solution)/shard_map/all_gather | solution.py:13
  473.6 13.6 reduce_sum.149
  496.2 5.8 fusion.119
  502.0 5.8 fusion.120
  507.8 12.3 multiply_convert_fusion.2
  524.4 6.2 convolution_add_fusion
  534.0 6.7 slice.611
  540.7 6.2 slice.618
  547.0 6.3 slice.609
  553.2 8.9 slice.612
  562.1 8.9 slice.619
  571.0 9.2 slice.610
  584.3 66.0 %all-reduce.75.cloned.1.call-done = f32[1024,1536]{1,0:T(8,128)} async-done(((f32[1024,1536]{1,0:T(8,128)}), f32[1024,1536]{1,0:T(8,128)}) %all-reduce.75.cloned.1.call-update) | async-done | bytes 6291472 | tf_op jit(solution)/shard_map/psum | solution.py:169
  650.3 6.3 multiply_reduce_fusion
  667.4 6.2 slice.613
  673.6 6.2 slice.615
  679.8 8.9 slice.614
  688.7 8.9 slice.616
  809.3 6.2 slice.687
  879.4 8.5 pad.189
  887.9 9.1 slice.688
  900.7 8.5 pad.188
  913.3 16.6 rev.2
  929.9 8.4 multiply_reduce_fusion.5
  951.9 6.7 multiply_reduce_fusion.9
  968.9 6.7 fusion.24
  975.7 5.9 fusion.86
  981.6 9.9 fusion.123
  991.6 10.0 fusion.124
  1002.1 9.9 fusion.125
  1019.8 6.1 fusion.122
  1026.0 7.3 add_convert_fusion
  1033.4 7.3 convolution_convert_fusion
  1047.2 73.4 %reduce-scatter.23.cloned.1.call-done = f32[64,1536]{1,0:T(8,128)} async-done(((f32[512,1536]{1,0:T(8,128)}), f32[64,1536]{1,0:T(8,128)}) %reduce-scatter.23.cloned.1.call-update) | async-done | bytes 393232 | tf_op jit(solution)/shard_map/reduce_scatter | solution.py:222
  1122.3 75.4 %reduce-scatter.15.cloned.1.call-done = f32[192,512]{1,0:T(8,128)} async-done(((f32[1536,512]{1,0:T(8,128)}), f32[192,512]{1,0:T(8,128)}) %reduce-scatter.15.cloned.1.call-update) | async-done | bytes 393232 | tf_op jit(solution)/shard_map/reduce_scatter | solution.py:211
  1199.5 130.7 %reduce-scatter.25.cloned.1.call-done = f32[192,1152]{1,0:T(8,128)} async-done(((f32[1536,1152]{1,0:T(8,128)}), f32[192,1152]{1,0:T(8,128)}) %reduce-scatter.25.cloned.1.call-update) | async-done | bytes 884752 | tf_op jit(solution)/shard_map/reduce_scatter | solution.py:224
  1332.4 130.5 %reduce-scatter.27.cloned.1.call-done = f32[192,1152]{1,0:T(8,128)} async-done(((f32[1536,1152]{1,0:T(8,128)}), f32[192,1152]{1,0:T(8,128)}) %reduce-scatter.27.cloned.1.call-update) | async-done | bytes 884752 | tf_op jit(solution)/shard_map/reduce_scatter | solution.py:225
  1464.9 130.3 %reduce-scatter.29.cloned.1.call-done = f32[1152,192]{0,1:T(8,128)} async-done(((f32[1152,1536]{0,1:T(8,128)}), f32[1152,192]{0,1:T(8,128)}) %reduce-scatter.29.cloned.1.call-update) | async-done | bytes 884752 | tf_op jit(solution)/shard_map/reduce_scatter | solution.py:226
  1605.9 54.5 %reduce-scatter.33.cloned.1.call-done = f32[64,4]{1,0:T(8,128)} async-done(((f32[512,4]{1,0:T(8,128)}), f32[64,4]{1,0:T(8,128)}) %reduce-scatter.33.cloned.1.call-update) | async-done | bytes 1040
  1661.2 18.6 all-gather.1
  1680.5 45.3 %reduce-scatter.19.cloned.1.call-done = f32[4,16,128]{2,1,0:T(8,128)} async-done(((f32[4,128,128]{2,1,0:T(8,128)}), f32[4,16,128]{2,1,0:T(8,128)}) %reduce-scatter.19.cloned.1.call-update) | async-done | bytes 32784 | tf_op jit(solution)/shard_map/reduce_scatter | solution.py:217
  1726.5 30.6 %all_gather.74 = bf16[4,128,128]{2,1,0:T(8,128)(2,1)S(1)} all-gather(bf16[4,16,128]{2,1,0:T(8,128)(2,1)S(1)} %convert_element_type.250), channel_id=1, replica_groups=mesh['dp'=8,'tensor'=4] {'dp'}, dimensions={1}, use_global_device_ids=true | all-gather | bytes 147456 | tf_op jit(solution)/shard_map/all_gather | solution.py:250
  1757.8 33.4 %reduce-scatter.21.cloned.1.call-done = f32[4,16,128]{2,1,0:T(8,128)} async-done(((f32[4,128,128]{2,1,0:T(8,128)}), f32[4,16,128]{2,1,0:T(8,128)}) %reduce-scatter.21.cloned.1.call-update) | async-done | bytes 32784 | tf_op jit(solution)/shard_map/reduce_scatter | solution.py:219
  1792.0 30.8 %all_gather.76 = bf16[4,128,128]{2,1,0:T(8,128)(2,1)S(1)} all-gather(bf16[4,16,128]{2,1,0:T(8,128)(2,1)S(1)} %convert_element_type.255), channel_id=1, replica_groups=mesh['dp'=8,'tensor'=4] {'dp'}, dimensions={1}, use_global_device_ids=true | all-gather | bytes 147456 | tf_op jit(solution)/shard_map/all_gather | solution.py:256
  1823.5 38.1 %all-reduce.77.cloned.1.call-done = bf16[1024,1536]{1,0:T(8,128)(2,1)} async-done(((bf16[1024,1536]{1,0:T(8,128)(2,1)}), bf16[1024,1536]{1,0:T(8,128)(2,1)}) %all-reduce.77.cloned.1.call-update) | async-done | bytes 3145744 | tf_op jit(solution)/shard_map/psum | solution.py:206
  1861.6 6.8 fusion
  1868.4 38.4 %all-reduce.70 = (bf16[1536]{0:T(1024)(128)(2,1)}, bf16[512]{0:T(512)(128)(2,1)}, bf16[512]{0:T(512)(128)(2,1)}, bf16[512]{0:T(512)(128)(2,1)}, bf16[512]{0:T(51...) all-reduce(f32[1536]{0:T(1024)} %get-tuple-element.116, ...), channel_id=4, replica_groups=mesh['dp'=8,'tensor'=4] {'dp'}, use_global_device_ids=true, to_apply=%region_9.10.clone | all-reduce | flops 6144 | bytes 36864
  1926.3 34.5 %all-reduce.71 = (bf16[1536]{0:T(1024)(128)(2,1)}, bf16[512]{0:T(512)(128)(2,1)}, bf16[512]{0:T(512)(128)(2,1)}, bf16[512]{0:T(512)(128)(2,1)}, bf16[512]{0:T(51...) all-reduce(bf16[1536]{0:T(1024)(128)(2,1)S(1)} %dynamic-update-slic, ...), channel_id=1, replica_groups=mesh['dp'=8,'tensor'=4] {'dp'}, use_global_device_ids=true, to_apply=%add.54 | all-reduce | flops 6144 | bytes 24576
  1984.1 10.3 all-gather.20.cloned.1.call-done
  1997.9 41.1 %all-gather.16.cloned.1.call-done = bf16[1536,512]{1,0:T(8,128)(2,1)} async-done(((bf16[192,512]{1,0:T(8,128)(2,1)}), bf16[1536,512]{1,0:T(8,128)(2,1)}) %all-gather.16.cloned.1.call-update) | async-done | bytes 1572880 | tf_op jit(solution)/shard_map/all_gather | solution.py:232
  2042.6 61.7 %all-gather.22.cloned.1.call-done = bf16[1536,1152]{1,0:T(8,128)(2,1)} async-done(((bf16[192,1152]{1,0:T(8,128)(2,1)}), bf16[1536,1152]{1,0:T(8,128)(2,1)}) %all-gather.22.cloned.1.call-update) | async-done | bytes 3538960 | tf_op jit(solution)/shard_map/all_gather | solution.py:271
  2109.7 60.0 %all-gather.24.cloned.1.call-done = bf16[1536,1152]{1,0:T(8,128)(2,1)} async-done(((bf16[192,1152]{1,0:T(8,128)(2,1)}), bf16[1536,1152]{1,0:T(8,128)(2,1)}) %all-gather.24.cloned.1.call-update) | async-done | bytes 3538960 | tf_op jit(solution)/shard_map/all_gather | solution.py:274
  2175.1 60.1 %all-gather.26.cloned.1.call-done = bf16[1152,1536]{0,1:T(8,128)(2,1)} async-done(((bf16[1152,192]{0,1:T(8,128)(2,1)}), bf16[1152,1536]{0,1:T(8,128)(2,1)}) %all-gather.26.cloned.1.call-update) | async-done | bytes 3538960 | tf_op jit(solution)/shard_map/all_gather | solution.py:277
  2235.2 6.0 copy.116
  (526 shorter events, 563.5 us)
Async XLA Ops:
  7.2 500.6 %copy-start = (bf16[1152,1536]{1,0:T(8,128)(2,1)S(1)}, bf16[1152,1536]{1,0:T(8,128)(2,1)}, u32[]{:S(2)}) copy-start(bf16[1152,1536]{1,0:T(8,128)(2,1)} %param.39) | copy-start | bytes 10616836
  7.2 33.6 %all-gather.12.cloned.1.call-start = ((), (), s32[]{:S(2)}) async-start(), calls=%async_computation.10 | async-start | bytes 3932160 | tf_op jit(solution)/shard_map/all_gather | solution.py:114
  7.9 465.6 %all-gather.28.cloned.1.call-start = ((), (), s32[]{:S(2)}) async-start(), calls=%async_computation.28 | async-start | bytes 31457280 | tf_op jit(solution)/shard_map/all_gather | solution.py:13
  13.9 51.3 %copy-start.15 = (f32[512]{0:T(512)}, f32[512]{0:T(512)S(1)}, u32[]{:S(2)}) copy-start(f32[512]{0:T(512)S(1)} %convert_element_type.215) | copy-start | bytes 6148
  21.2 26.3 %copy-start.17 = (f32[1024]{0:T(1024)}, f32[1024]{0:T(1024)S(1)}, u32[]{:S(2)}) copy-start(f32[1024]{0:T(1024)S(1)} %get-tuple-element.209) | copy-start | bytes 12292
  21.2 26.3 %copy-start.19 = (f32[1024]{0:T(1024)}, f32[1024]{0:T(1024)S(1)}, u32[]{:S(2)}) copy-start(f32[1024]{0:T(1024)S(1)} %get-tuple-element.214) | copy-start | bytes 12292
  21.2 26.3 %copy-start.21 = (f32[1024]{0:T(1024)}, f32[1024]{0:T(1024)S(1)}, u32[]{:S(2)}) copy-start(f32[1024]{0:T(1024)S(1)} %get-tuple-element.215) | copy-start | bytes 12292
  207.7 13.9 copy-start.45
  207.7 13.9 copy-start.59
  234.8 18.4 copy-start.55
  253.2 11.0 copy-start.53
  296.4 8.6 copy-start.24
  296.5 8.6 copy-start.31
  296.5 8.6 copy-start.64
  305.1 9.1 copy-start.74
  318.6 189.1 %all-gather.14.cloned.1.call-start = ((), (), s32[]{:S(2)}) async-start(), calls=%async_computation.11 | async-start | bytes 3932160 | tf_op jit(solution)/shard_map/all_gather | solution.py:157
  319.4 330.9 %all-reduce.75.cloned.1.call-start = ((), (), s32[]{:S(2)}) async-start(), calls=%async_computation.12 | async-start | bytes 12582912 | tf_op jit(solution)/shard_map/psum | solution.py:169
  491.9 4.3 copy-start.70
  496.2 5.8 copy-start.12
  496.2 5.8 copy-start.72
  507.8 12.3 copy-start.71
  520.1 4.3 copy-start.79
  520.1 4.3 copy-start.78
  520.1 4.3 copy-start.73
  530.6 514.8 %reduce-scatter.17.cloned.1.call-start = ((), (), s32[]{:S(2)}) async-start(), calls=%async_computation.16 | async-start | bytes 3538944 | tf_op jit(solution)/shard_map/reduce_scatter | solution.py:213
  650.3 6.4 copy-start.8
  650.3 7.4 copy-start.11
  657.6 4.6 copy-start.77
  661.6 5.8 copy-start.7
  800.6 16.2 copy-start.46
  800.6 16.2 copy-start.60
  830.0 18.4 copy-start.56
  848.4 11.0 copy-start.54
  913.3 16.6 copy-start.16
  913.3 16.6 copy-start.34
  913.3 16.6 copy-start.36
  913.3 16.6 copy-start.48
  929.9 8.4 copy-start.61
  929.9 9.0 copy-start.4
  951.9 6.8 copy-start.2
  951.9 6.8 copy-start.18
  951.9 6.7 copy-start.20
  968.6 151.9 %reduce-scatter.23.cloned.1.call-start = ((), (), s32[]{:S(2)}) async-start(), calls=%async_computation.20 | async-start | bytes 3538944 | tf_op jit(solution)/shard_map/reduce_scatter | solution.py:222
  975.6 222.2 %reduce-scatter.15.cloned.1.call-start = ((), (), s32[]{:S(2)}) async-start(), calls=%async_computation.14 | async-start | bytes 3538944 | tf_op jit(solution)/shard_map/reduce_scatter | solution.py:211
  981.6 348.7 %reduce-scatter.25.cloned.1.call-start = ((), (), s32[]{:S(2)}) async-start(), calls=%async_computation.22 | async-start | bytes 7962624 | tf_op jit(solution)/shard_map/reduce_scatter | solution.py:224
  991.6 471.3 %reduce-scatter.27.cloned.1.call-start = ((), (), s32[]{:S(2)}) async-start(), calls=%async_computation.24 | async-start | bytes 7962624 | tf_op jit(solution)/shard_map/reduce_scatter | solution.py:225
  1001.6 593.6 %reduce-scatter.29.cloned.1.call-start = ((), (), s32[]{:S(2)}) async-start(), calls=%async_computation.26 | async-start | bytes 7962624 | tf_op jit(solution)/shard_map/reduce_scatter | solution.py:226
  1012.0 648.4 %reduce-scatter.33.cloned.1.call-start = ((), (), s32[]{:S(2)}) async-start(), calls=%async_computation.30 | async-start | bytes 294912
  1014.3 711.5 %reduce-scatter.19.cloned.1.call-start = ((), (), s32[]{:S(2)}) async-start(), calls=%async_computation.18 | async-start | bytes 294912 | tf_op jit(solution)/shard_map/reduce_scatter | solution.py:217
  1017.0 774.2 %reduce-scatter.21.cloned.1.call-start = ((), (), s32[]{:S(2)}) async-start(), calls=%async_computation.19 | async-start | bytes 294912 | tf_op jit(solution)/shard_map/reduce_scatter | solution.py:219
  1025.9 835.7 %all-reduce.77.cloned.1.call-start = ((), (), s32[]{:S(2)}) async-start(), calls=%async_computation.13 | async-start | bytes 6291456 | tf_op jit(solution)/shard_map/psum | solution.py:206
  1033.3 942.1 %reduce-scatter.31.cloned.1.call-start = ((), (), s32[]{:S(2)}) async-start(), calls=%async_computation.29 | async-start | bytes 3932160
  1045.3 935.2 %all-gather.18.cloned.1.call-start = ((), (), s32[]{:S(2)}) async-start(), calls=%async_computation.17 | async-start | bytes 1769472 | tf_op jit(solution)/shard_map/all_gather | solution.py:238
  1047.1 947.3 %all-gather.20.cloned.1.call-start = ((), (), s32[]{:S(2)}) async-start(), calls=%async_computation.21 | async-start | bytes 1769472 | tf_op jit(solution)/shard_map/all_gather | solution.py:265
  1122.3 916.8 %all-gather.16.cloned.1.call-start = ((), (), s32[]{:S(2)}) async-start(), calls=%async_computation.15 | async-start | bytes 1769472 | tf_op jit(solution)/shard_map/all_gather | solution.py:232
  1199.5 904.8 %all-gather.22.cloned.1.call-start = ((), (), s32[]{:S(2)}) async-start(), calls=%async_computation.23 | async-start | bytes 3981312 | tf_op jit(solution)/shard_map/all_gather | solution.py:271
  1332.3 265.0 %copy-start.63 = (u32[32]{0:T(128)S(1)}, u32[32]{0:T(128)}, u32[]{:S(2)}) copy-start(u32[32]{0:T(128)} %constant.193) | copy-start | bytes 388
  1332.3 837.3 %all-gather.24.cloned.1.call-start = ((), (), s32[]{:S(2)}) async-start(), calls=%async_computation.25 | async-start | bytes 3981312 | tf_op jit(solution)/shard_map/all_gather | solution.py:274
  1464.8 770.4 %all-gather.26.cloned.1.call-start = ((), (), s32[]{:S(2)}) async-start(), calls=%async_computation.27 | async-start | bytes 3981312 | tf_op jit(solution)/shard_map/all_gather | solution.py:277
  1823.5 44.9 %copy-start.29 = (f32[1536]{0:T(1024)S(1)}, f32[1536]{0:T(1024)}, u32[]{:S(2)}) copy-start(f32[1536]{0:T(1024)} %get-tuple-element.114) | copy-start | bytes 18436
  1823.5 147.4 %copy-start.28 = (f32[1024]{0:T(1024)S(1)}, f32[1024]{0:T(1024)}, u32[]{:S(2)}) copy-start(f32[1024]{0:T(1024)} %copy-done.27) | copy-start | bytes 12292
  1823.5 148.1 %copy-start.26 = (f32[1024]{0:T(1024)S(1)}, f32[1024]{0:T(1024)}, u32[]{:S(2)}) copy-start(f32[1024]{0:T(1024)} %copy-done.23) | copy-start | bytes 12292
  1916.6 5.2 copy-start.68
  1917.5 6.6 copy-start.69
  (37 other events, 93.8 us)
Sparse Core Ops, SparseCore 0:
  9.6 31.1 all-gather.11
  318.8 154.7 all-gather.27
  475.2 28.4 all-gather.13
  530.7 119.5 all-reduce.74
  968.8 74.9 reduce-scatter.16
  1047.2 73.3 reduce-scatter.22
  1124.1 73.5 reduce-scatter.14
  1202.0 128.2 reduce-scatter.24
  1334.5 128.2 reduce-scatter.26
  1466.9 128.2 reduce-scatter.28
  1599.1 61.1 reduce-scatter.32
  1664.1 61.5 reduce-scatter.18
  1729.7 61.5 reduce-scatter.20
  1794.1 67.4 all-reduce.76
  1864.5 37.9 reduce-scatter.30
  1905.2 44.4 all-gather.17
  1951.7 42.7 all-gather.19
  1996.5 42.5 all-gather.15
  2041.3 62.9 all-gather.21
  2106.3 63.3 all-gather.23
  2171.8 63.3 all-gather.25
